TPU v7x, 32 devices: a whole 2x2x4 slice. The times are simulated.
32 devices in a mesh: dp: 2 (over core), row: 4 (over y, x), col: 4 (over z).
Axes of the slice: x: 2, y: 2, z: 4, core: 2. Of those that a mesh axis runs over, the one named last changes fastest.
Arguments:
- inputs: bfloat16 [32768, 768], P(('dp', 'row', 'col')), may hold values from -6 to 6
- segment_ids: int32 [32768], P(('dp', 'row', 'col')), may hold values from 0 to 3, as said below
- query_weight: bfloat16 [768, 768], P('row', 'col'), may hold values from -0.21875 to 0.21875
- key_weight: bfloat16 [768, 768], P('row', 'col'), may hold values from -0.21875 to 0.21875
- value_weight: bfloat16 [768, 768], P('row', 'col'), may hold values from -0.21875 to 0.21875
- output_weight: bfloat16 [768, 768], P('row', 'col'), may hold values from -1.75 to 1.75
- gate_weight: bfloat16 [768, 2048], P('row', 'col'), may hold values from -0.21875 to 0.21875
- up_weight: bfloat16 [768, 2048], P('row', 'col'), may hold values from -0.21875 to 0.21875
- down_weight: bfloat16 [2048, 768], P('row', 'col'), may hold values from -0.125 to 0.125
- first_gain: bfloat16 [768], P(('row', 'col')), may hold values from 0.099609375 to 1.8984375
- second_gain: bfloat16 [768], P(('row', 'col')), may hold values from 0.099609375 to 1.8984375
- cotangent: bfloat16 [32768, 768], P(('dp', 'row', 'col')), may hold values from -6 to 6
Outputs:
- layer_out: bfloat16 [32768, 768], P(('dp', 'row', 'col'))
- input_grad: bfloat16 [32768, 768], P(('dp', 'row', 'col'))
- query_grad: float32 [768, 768], P('row', 'col')
- key_grad: float32 [768, 768], P('row', 'col')
- value_grad: float32 [768, 768], P('row', 'col')
- output_grad: float32 [768, 768], P('row', 'col')
- gate_grad: float32 [768, 2048], P('row', 'col')
- up_grad: float32 [768, 2048], P('row', 'col')
- down_grad: float32 [2048, 768], P('row', 'col')
- first_gain_grad: float32 [768], P(('row', 'col'))
- second_gain_grad: float32 [768], P(('row', 'col'))
Inputs may be any that keep to these rules, and one draw needn't show every extreme that they name: `segment_ids`: within each aligned block of 1024 tokens the ids number that block's sequences 0, 1, ... in order; a block holds 1, 2 or 4 sequences of equal length, and each of the three cases occurs in some block.
All inputs are finite; a program needn't handle non-finite values.
Results may differ from a plain program's by a relative error of at most 0.017.
Values may be sent and summed in bfloat16 or wider, within the bound.
No kernel may reach another device: no remote copies, remote signals or barrier semaphores. Data moves between devices by JAX's collectives and lax.ppermute only.
A program may use at most 192 MiB of HBM per device.

v0:
```python
import jax
import jax.numpy as jnp
from jax import lax
from jax.sharding import PartitionSpec as P

HEAD_DIM = 64
EPSILON = 1e-06
ROPE_BASE = 10000.0
NEGATIVE = -1e30


def for_sending(value):

    def short(part):
        return part.astype(jnp.bfloat16) if part.dtype == jnp.float32 else part

    return jax.tree.map(short, value)


def assemble(stack, grid_rows, grid_cols):
    height = stack.shape[1]
    breadth = stack.shape[2]
    return (
        stack.reshape(grid_rows, grid_cols, height, breadth)
        .transpose(0, 2, 1, 3)
        .reshape(grid_rows * height, grid_cols * breadth)
    )


def disassemble(whole, grid_rows, grid_cols):
    height = whole.shape[0] // grid_rows
    breadth = whole.shape[1] // grid_cols
    return (
        whole.reshape(grid_rows, height, grid_cols, breadth)
        .transpose(0, 2, 1, 3)
        .reshape(grid_rows * grid_cols, height, breadth)
    )


def fetch_attention(
    query_weight, key_weight, value_weight, output_weight, first_gain, grid_rows, grid_cols
):
    pieces = (
        lax.all_gather(query_weight[None], ("row", "col"), axis=0, tiled=True),
        lax.all_gather(key_weight[None], ("row", "col"), axis=0, tiled=True),
        lax.all_gather(value_weight[None], ("row", "col"), axis=0, tiled=True),
        lax.all_gather(output_weight[None], ("row", "col"), axis=0, tiled=True),
        lax.all_gather(first_gain[None], ("row", "col"), axis=0, tiled=True),
    )
    wholes = tuple((assemble(piece, grid_rows, grid_cols) for piece in pieces[:4]))
    return wholes + (pieces[4].reshape(-1).astype(jnp.float32),)


def fetch_feedforward(gate_weight, up_weight, down_weight, second_gain, grid_rows, grid_cols):
    pieces = (
        lax.all_gather(gate_weight[None], ("row", "col"), axis=0, tiled=True),
        lax.all_gather(up_weight[None], ("row", "col"), axis=0, tiled=True),
        lax.all_gather(down_weight[None], ("row", "col"), axis=0, tiled=True),
        lax.all_gather(second_gain[None], ("row", "col"), axis=0, tiled=True),
    )
    wholes = tuple((assemble(piece, grid_rows, grid_cols) for piece in pieces[:3]))
    return wholes + (pieces[3].reshape(-1).astype(jnp.float32),)


def rms_scale(values):
    return lax.rsqrt(jnp.mean(values * values, axis=-1, keepdims=True) + EPSILON)


def rotate(values, cosine, sine):
    half = values.shape[-1] // 2
    front = values[..., :half]
    behind = values[..., half:]
    return jnp.concatenate(
        [front * cosine - behind * sine, behind * cosine + front * sine], axis=-1
    )


def split_heads(values, head_count):
    return values.reshape(values.shape[0], head_count, -1).transpose(1, 0, 2)


def join_heads(values):
    return values.transpose(1, 0, 2).reshape(values.shape[1], -1)


def attend_head(operands, allowed, score_scale):
    queries, keys, values = operands
    scores = jnp.einsum("qd,kd->qk", queries, keys, preferred_element_type=jnp.float32)
    logits = jnp.where(allowed, scores * score_scale, NEGATIVE)
    row_top = jnp.max(logits, axis=1, keepdims=True)
    weights = jnp.exp(logits - row_top)
    row_total = jnp.sum(weights, axis=1, keepdims=True)
    probs_low = (weights / row_total).astype(jnp.bfloat16)
    context = jnp.dot(probs_low, values, preferred_element_type=jnp.float32)
    return (context, row_top[:, 0], row_total[:, 0])


def attend_back(operands, allowed, score_scale):
    queries, keys, values, row_top, row_total, grad_context = operands
    scores = jnp.einsum("qd,kd->qk", queries, keys, preferred_element_type=jnp.float32)
    logits = jnp.where(allowed, scores * score_scale, NEGATIVE)
    probs = jnp.exp(logits - row_top[:, None]) / row_total[:, None]
    probs_low = probs.astype(jnp.bfloat16)
    grad_vals = jnp.einsum("qk,qd->kd", probs_low, grad_context, preferred_element_type=jnp.float32)
    grad_probs = jnp.einsum("qd,kd->qk", grad_context, values, preferred_element_type=jnp.float32)
    inner = jnp.sum(probs * grad_probs, axis=1, keepdims=True)
    grad_scores = (jnp.where(allowed, probs * (grad_probs - inner), 0.0) * score_scale).astype(
        jnp.bfloat16
    )
    grad_qrot = jnp.dot(grad_scores, keys, preferred_element_type=jnp.float32)
    grad_krot = jnp.einsum("qk,qd->kd", grad_scores, queries, preferred_element_type=jnp.float32)
    return (grad_qrot, grad_krot, grad_vals)


def weight_term(left, right):
    return jnp.einsum("ta,tb->ab", left, right, preferred_element_type=jnp.float32)


def back_product(grad, weight):
    return jnp.einsum("tb,ab->ta", grad, weight, preferred_element_type=jnp.float32)


def on_device(
    inputs,
    segment_ids,
    query_weight,
    key_weight,
    value_weight,
    output_weight,
    gate_weight,
    up_weight,
    down_weight,
    first_gain,
    second_gain,
    cotangent,
):
    grid_rows = lax.axis_size("row")
    grid_cols = lax.axis_size("col")
    token_count, model_width = inputs.shape
    head_count = model_width // HEAD_DIM
    score_scale = HEAD_DIM ** (-0.5)
    token_index = jnp.arange(token_count, dtype=jnp.int32)
    same_seq = segment_ids[:, None] == segment_ids[None, :]
    allowed = same_seq & (token_index[None, :] <= token_index[:, None])
    starts = jnp.min(jnp.where(same_seq, token_index[None, :], token_count), axis=1)
    positions = (token_index - starts).astype(jnp.float32)
    frequencies = ROPE_BASE ** (-2.0 * jnp.arange(HEAD_DIM // 2, dtype=jnp.float32) / HEAD_DIM)
    phases = positions[:, None] * frequencies[None, :]
    cosine = jnp.cos(phases)[:, None, :]
    sine = jnp.sin(phases)[:, None, :]
    w_query, w_key, w_value, w_output, gain_one = fetch_attention(
        query_weight, key_weight, value_weight, output_weight, first_gain, grid_rows, grid_cols
    )
    query_flat = jnp.dot(inputs, w_query, preferred_element_type=jnp.float32)
    key_flat = jnp.dot(inputs, w_key, preferred_element_type=jnp.float32)
    value_flat = jnp.dot(inputs, w_value, preferred_element_type=jnp.float32)
    queries = rotate(query_flat.reshape(token_count, head_count, HEAD_DIM), cosine, sine).astype(
        jnp.bfloat16
    )
    keys = rotate(key_flat.reshape(token_count, head_count, HEAD_DIM), cosine, sine).astype(
        jnp.bfloat16
    )
    query_heads = queries.transpose(1, 0, 2)
    key_heads = keys.transpose(1, 0, 2)
    value_heads = split_heads(value_flat.astype(jnp.bfloat16), head_count)

    def head_forward(operands):
        return attend_head(operands, allowed, score_scale)

    contexts, row_tops, row_totals = lax.map(head_forward, (query_heads, key_heads, value_heads))
    context = join_heads(contexts).astype(jnp.bfloat16)
    first_sum = inputs.astype(jnp.float32) + jnp.dot(
        context, w_output, preferred_element_type=jnp.float32
    )
    scale_one = rms_scale(first_sum)
    normed_one = first_sum * scale_one
    normed = normed_one * gain_one
    hidden_in = normed.astype(jnp.bfloat16)
    w_gate, w_up, w_down, gain_two = fetch_feedforward(
        gate_weight, up_weight, down_weight, second_gain, grid_rows, grid_cols
    )
    gate_act = jnp.dot(hidden_in, w_gate, preferred_element_type=jnp.float32)
    up_act = jnp.dot(hidden_in, w_up, preferred_element_type=jnp.float32)
    gate_sigmoid = jax.nn.sigmoid(gate_act)
    hidden = (gate_act * gate_sigmoid * up_act).astype(jnp.bfloat16)
    second_sum = normed + jnp.dot(hidden, w_down, preferred_element_type=jnp.float32)
    scale_two = rms_scale(second_sum)
    normed_two = second_sum * scale_two
    layer_out = (normed_two * gain_two).astype(jnp.bfloat16)
    grad_out = cotangent.astype(jnp.float32)
    gain_two_term = jnp.sum(grad_out * normed_two, axis=0)
    grad_norm_two = grad_out * gain_two
    grad_second = scale_two * (
        grad_norm_two - normed_two * jnp.mean(grad_norm_two * normed_two, axis=-1, keepdims=True)
    )
    grad_branch_two = grad_second.astype(jnp.bfloat16)
    w_gate, w_up, w_down, gain_two = fetch_feedforward(
        gate_weight, up_weight, down_weight, second_gain, grid_rows, grid_cols
    )
    down_term = weight_term(hidden, grad_branch_two)
    grad_hidden = back_product(grad_branch_two, w_down)
    grad_gate = (
        grad_hidden * up_act * (gate_sigmoid + gate_act * gate_sigmoid * (1.0 - gate_sigmoid))
    ).astype(jnp.bfloat16)
    grad_up = (grad_hidden * gate_act * gate_sigmoid).astype(jnp.bfloat16)
    gate_term = weight_term(hidden_in, grad_gate)
    up_term = weight_term(hidden_in, grad_up)
    grad_normed = grad_second + back_product(grad_gate, w_gate) + back_product(grad_up, w_up)
    gain_lanes = gain_two_term.reshape(grid_rows * grid_cols, -1)
    feed_shares = (
        lax.psum_scatter(
            disassemble(gate_term, grid_rows, grid_cols),
            ("row", "col"),
            scatter_dimension=0,
            tiled=True,
        ),
        lax.psum_scatter(
            disassemble(up_term, grid_rows, grid_cols),
            ("row", "col"),
            scatter_dimension=0,
            tiled=True,
        ),
        lax.psum_scatter(
            disassemble(down_term, grid_rows, grid_cols),
            ("row", "col"),
            scatter_dimension=0,
            tiled=True,
        ),
        lax.psum_scatter(gain_lanes, ("row", "col"), scatter_dimension=0, tiled=True),
    )
    gain_one_term = jnp.sum(grad_normed * normed_one, axis=0)
    grad_norm_one = grad_normed * gain_one
    grad_first = scale_one * (
        grad_norm_one - normed_one * jnp.mean(grad_norm_one * normed_one, axis=-1, keepdims=True)
    )
    grad_branch_one = grad_first.astype(jnp.bfloat16)
    w_query, w_key, w_value, w_output, gain_one = fetch_attention(
        query_weight, key_weight, value_weight, output_weight, first_gain, grid_rows, grid_cols
    )
    output_term = weight_term(context, grad_branch_one)
    grad_context = back_product(grad_branch_one, w_output).astype(jnp.bfloat16)

    def head_backward(operands):
        return attend_back(operands, allowed, score_scale)

    grad_qrots, grad_krots, grad_valss = lax.map(
        head_backward,
        (
            query_heads,
            key_heads,
            value_heads,
            row_tops,
            row_totals,
            split_heads(grad_context, head_count),
        ),
    )
    grad_query = (
        rotate(grad_qrots.transpose(1, 0, 2), cosine, -sine)
        .reshape(token_count, model_width)
        .astype(jnp.bfloat16)
    )
    grad_key = (
        rotate(grad_krots.transpose(1, 0, 2), cosine, -sine)
        .reshape(token_count, model_width)
        .astype(jnp.bfloat16)
    )
    grad_value = join_heads(grad_valss).astype(jnp.bfloat16)
    query_term = weight_term(inputs, grad_query)
    key_term = weight_term(inputs, grad_key)
    value_term = weight_term(inputs, grad_value)
    input_grad = (
        grad_first
        + back_product(grad_query, w_query)
        + back_product(grad_key, w_key)
        + back_product(grad_value, w_value)
    ).astype(jnp.bfloat16)
    attention_parts = (
        disassemble(query_term, grid_rows, grid_cols),
        disassemble(key_term, grid_rows, grid_cols),
        disassemble(value_term, grid_rows, grid_cols),
        disassemble(output_term, grid_rows, grid_cols),
    )
    first_lanes = gain_one_term.reshape(grid_rows * grid_cols, -1)
    attention_shares = lax.psum_scatter(
        attention_parts + (first_lanes,), ("row", "col"), scatter_dimension=0, tiled=True
    )
    shares = attention_shares[:4] + feed_shares[:3] + (attention_shares[4], feed_shares[3])
    summed = jax.tree.map(
        lambda part: part.astype(jnp.float32),
        lax.psum(for_sending(tuple((share[0] for share in shares))), "dp"),
    )
    return (
        layer_out,
        input_grad,
        summed[0],
        summed[1],
        summed[2],
        summed[3],
        summed[4],
        summed[5],
        summed[6],
        summed[7],
        summed[8],
    )


def solution(mesh):
    placed = (
        P(("dp", "row", "col"), None),
        P(("dp", "row", "col")),
        P("row", "col"),
        P("row", "col"),
        P("row", "col"),
        P("row", "col"),
        P("row", "col"),
        P("row", "col"),
        P("row", "col"),
        P(("row", "col")),
        P(("row", "col")),
        P(("dp", "row", "col"), None),
    )
    return jax.shard_map(
        on_device,
        mesh=mesh,
        in_specs=placed,
        out_specs=(
            P(("dp", "row", "col"), None),
            P(("dp", "row", "col"), None),
            P("row", "col"),
            P("row", "col"),
            P("row", "col"),
            P("row", "col"),
            P("row", "col"),
            P("row", "col"),
            P("row", "col"),
            P(("row", "col")),
            P(("row", "col")),
        ),
        check_vma=False,
    )
```

profile of v0, /device:TPU:0, one launch (start us, length us, event | category | flops | bytes accessed | tf_op | source)
XLA Modules:
  0.0 1591.9 jit_solution(5571109859749134416)
XLA Ops:
  18.3 44.6 %all-reduce.5 = (bf16[768]{0:T(1024)(128)(2,1)S(1)}, bf16[768]{0:T(1024)(128)(2,1)S(1)}) all-reduce(bf16[768]{0:T(1024)(128)(2,1)S(1)} %dynamic-update-slice, bf16[768]{0:T(1024)(128)(2,1)S(1)} %dynamic-update-slice.1), channel_id=6, replica_groups=mesh['dp'=2,'row'=4,'col'=4] {'row','col'}, use_global_device_ids=true, to_apply=%add | all-reduce | flops 1536 | bytes 6144
  65.8 5.8 all-gather.19.cloned.1.call-done
  81.2 50.0 %all-gather.17.cloned.1.call-done = bf16[3072,192]{1,0:T(8,128)(2,1)} async-done(((bf16[192,192]{1,0:T(8,128)(2,1)}), bf16[3072,192]{1,0:T(8,128)(2,1)}) %all-gather.17.cloned.1.call-update) | async-done | bytes 1179664 | tf_op jit(solution)/shard_map/all_gather | solution.py:44
  146.2 44.5 %all-gather.21.cloned.1.call-done = bf16[3072,192]{1,0:T(8,128)(2,1)} async-done(((bf16[192,192]{1,0:T(8,128)(2,1)}), bf16[3072,192]{1,0:T(8,128)(2,1)}) %all-gather.21.cloned.1.call-update) | async-done | bytes 1179664 | tf_op jit(solution)/shard_map/all_gather | solution.py:46
  203.5 56.9 %while.32 = (s32[]{:T(128)}, bf16[12,1024,64]{1,2,0:T(8,128)(2,1)S(1)}, f32[12,1024]{1,0:T(8,128)S(1)}, f32[12,1024]{1,0:T(8,128)S(1)}, bf16[12,1024,64]{2,1,0:T...) while((s32[]{:T(128)}, ...), condition=%wide.region_4.5_spmd.clone.clone, body=%wide.region_1.4_spmd.clone.sunk.clone | while | flops 279967744 | bytes 13678685 | solution.py:170
  271.4 48.1 %all-gather.25.cloned.1.call-done = bf16[3072,512]{1,0:T(8,128)(2,1)} async-done(((bf16[192,512]{1,0:T(8,128)(2,1)}), bf16[3072,512]{1,0:T(8,128)(2,1)}) %all-gather.25.cloned.1.call-update) | async-done | bytes 3145744 | tf_op jit(solution)/shard_map/all_gather | solution.py:56
  326.6 62.2 %all-gather.27.cloned.1.call-done = bf16[3072,512]{1,0:T(8,128)(2,1)} async-done(((bf16[192,512]{1,0:T(8,128)(2,1)}), bf16[3072,512]{1,0:T(8,128)(2,1)}) %all-gather.27.cloned.1.call-update) | async-done | bytes 3145744 | tf_op jit(solution)/shard_map/all_gather | solution.py:57
  395.7 65.5 %all-gather.29.cloned.1.call-done = bf16[8192,192]{0,1:T(8,128)(2,1)} async-done(((bf16[512,192]{0,1:T(8,128)(2,1)}), bf16[8192,192]{0,1:T(8,128)(2,1)}) %all-gather.29.cloned.1.call-update) | async-done | bytes 3145744 | tf_op jit(solution)/shard_map/all_gather | solution.py:58
  461.2 6.6 reshape.314
  476.9 7.8 multiply_convert_fusion.3
  484.6 5.7 multiply_reduce_fusion.3
  493.2 12.6 multiply_convert_fusion.1
  505.8 5.5 fusion.74
  528.5 155.0 %while.33 = (s32[]{:T(128)}, f32[12,1024,64]{1,2,0:T(8,128)}, f32[12,1024,64]{1,2,0:T(8,128)}, bf16[12,1024,64]{1,2,0:T(8,128)(2,1)S(1)}, bf16[12,1024,64]{2,1,0...) while((s32[]{:T(128)}, f32[12,1024,64]{1,2,0:T(8,128)}, ...), condition=%wide.region_11.12_spmd.clone.clone, body=%wide.region_9.11_spmd.clone.sunk.clone | while | flops 689961984 | bytes 34129008 | solution.py:246
  692.7 4.9 reshape.317
  707.4 4.9 reshape.319
  729.2 9.4 fusion.58
  738.6 8.5 reshape.328
  747.0 7.4 copy.148
  755.9 7.4 fusion.79
  763.3 8.4 reshape.326
  771.7 7.3 copy.146
  779.1 7.5 fusion.78
  786.6 8.4 reshape.324
  795.0 7.7 copy.145
  803.5 74.5 %all-reduce.4 = (bf16[16,48]{1,0:T(8,128)(2,1)S(1)}, bf16[16,48]{1,0:T(8,128)(2,1)S(1)}) all-reduce(f32[16,48]{1,0:T(8,128)S(1)} %reshape.330, f32[16,48]{1,0:T(8,128)S(1)} %reshape.331), channel_id=18, replica_groups=mesh['dp'=2,'row'=4,'col'=4] {'row','col'}, use_global_device_ids=true, to_apply=%region_27.28.clone | all-reduce | flops 1536 | bytes 9216
  888.4 77.9 %reduce-scatter.10.cloned.1.call-done = f32[1,192,192]{2,1,0:T(8,128)} async-done(((f32[16,192,192]{2,1,0:T(8,128)}), f32[1,192,192]{2,1,0:T(8,128)}) %reduce-scatter.10.cloned.1.call-update) | async-done | bytes 147472 | tf_op jit(solution)/shard_map/reduce_scatter | solution.py:284
  967.9 133.2 %reduce-scatter.12.cloned.1.call-done = f32[1,192,192]{2,1,0:T(8,128)} async-done(((f32[16,192,192]{2,1,0:T(8,128)}), f32[1,192,192]{2,1,0:T(8,128)}) %reduce-scatter.12.cloned.1.call-update) | async-done | bytes 147472 | tf_op jit(solution)/shard_map/reduce_scatter | solution.py:284
  1102.7 148.1 %reduce-scatter.20.cloned.1.call-done = f32[1,512,192]{1,2,0:T(8,128)} async-done(((f32[16,512,192]{1,2,0:T(8,128)}), f32[1,512,192]{1,2,0:T(8,128)}) %reduce-scatter.20.cloned.1.call-update) | async-done | bytes 393232 | tf_op jit(solution)/shard_map/reduce_scatter | solution.py:223
  1252.5 148.5 %reduce-scatter.18.cloned.1.call-done = f32[1,192,512]{2,1,0:T(8,128)} async-done(((f32[16,192,512]{2,1,0:T(8,128)}), f32[1,192,512]{2,1,0:T(8,128)}) %reduce-scatter.18.cloned.1.call-update) | async-done | bytes 393232 | tf_op jit(solution)/shard_map/reduce_scatter | solution.py:217
  1402.7 148.1 %reduce-scatter.16.cloned.1.call-done = f32[1,192,512]{2,1,0:T(8,128)} async-done(((f32[16,192,512]{2,1,0:T(8,128)}), f32[1,192,512]{2,1,0:T(8,128)}) %reduce-scatter.16.cloned.1.call-update) | async-done | bytes 393232 | tf_op jit(solution)/shard_map/reduce_scatter | solution.py:211
  1556.9 7.9 add_convert_fusion
  (366 shorter events, 396.5 us)
Async XLA Ops:
  7.2 64.4 %all-gather.19.cloned.1.call-start = ((), (), s32[]{:S(2)}) async-start(), calls=%async_computation.15 | async-start | bytes 1671168 | tf_op jit(solution)/shard_map/all_gather | solution.py:45
  7.9 123.2 %all-gather.17.cloned.1.call-start = ((), (), s32[]{:S(2)}) async-start(), calls=%async_computation.14 | async-start | bytes 1671168 | tf_op jit(solution)/shard_map/all_gather | solution.py:44
  8.7 182.0 %all-gather.21.cloned.1.call-start = ((), (), s32[]{:S(2)}) async-start(), calls=%async_computation.16 | async-start | bytes 1671168 | tf_op jit(solution)/shard_map/all_gather | solution.py:46
  9.4 251.0 %all-gather.23.cloned.1.call-start = ((), (), s32[]{:S(2)}) async-start(), calls=%async_computation.17 | async-start | bytes 1671168 | tf_op jit(solution)/shard_map/all_gather | solution.py:47
  10.0 309.6 %all-gather.25.cloned.1.call-start = ((), (), s32[]{:S(2)}) async-start(), calls=%async_computation.18 | async-start | bytes 3342336 | tf_op jit(solution)/shard_map/all_gather | solution.py:56
  10.6 378.2 %all-gather.27.cloned.1.call-start = ((), (), s32[]{:S(2)}) async-start(), calls=%async_computation.19 | async-start | bytes 3342336 | tf_op jit(solution)/shard_map/all_gather | solution.py:57
  11.1 450.1 %all-gather.29.cloned.1.call-start = ((), (), s32[]{:S(2)}) async-start(), calls=%async_computation.20 | async-start | bytes 3342336 | tf_op jit(solution)/shard_map/all_gather | solution.py:58
  11.9 873.2 %reduce-scatter.14.cloned.1.call-start = ((), (), s32[]{:S(2)}) async-start(), calls=%async_computation.10 | async-start | bytes 3342336 | tf_op jit(solution)/shard_map/reduce_scatter | solution.py:284
  13.8 49.1 %copy-start.17 = (bf16[1024,768]{1,0:T(8,128)(2,1)S(1)}, bf16[1024,768]{1,0:T(8,128)(2,1)}, u32[]{:S(2)}) copy-start(bf16[1024,768]{1,0:T(8,128)(2,1)} %param.27) | copy-start | bytes 4718596
  62.9 453.1 %copy-start.36 = (f32[768]{0:T(1024)}, f32[768]{0:T(1024)S(1)}, u32[]{:S(2)}) copy-start(f32[768]{0:T(1024)S(1)} %convert_element_type.259) | copy-start | bytes 9220
  64.6 12.1 copy-start.18
  65.8 73.3 %copy-start.29 = (f32[1024,32]{0,1:T(8,128)}, f32[1024,32]{0,1:T(8,128)S(1)}, u32[]{:S(2)}) copy-start(f32[1024,32]{0,1:T(8,128)S(1)} %get-tuple-element.394) | copy-start | bytes 393220
  269.6 246.4 %copy-start = (f32[1024,768]{0,1:T(8,128)}, f32[1024,768]{0,1:T(8,128)S(1)}, u32[]{:S(2)}) copy-start(f32[1024,768]{0,1:T(8,128)S(1)} %get-tuple-element.398) | copy-start | bytes 9437188
  269.6 246.4 %copy-start.38 = (f32[1024]{0:T(1024)}, f32[1024]{0:T(1024)S(1)}, u32[]{:S(2)}) copy-start(f32[1024]{0:T(1024)S(1)} %add_rsqrt_fusion.1) | copy-start | bytes 12292
  490.3 21.1 %copy-start.13 = (f32[1024,768]{0,1:T(8,128)}, f32[1024,768]{0,1:T(8,128)S(1)}, u32[]{:S(2)}) copy-start(f32[1024,768]{0,1:T(8,128)S(1)} %get-tuple-element.402) | copy-start | bytes 9437188
  493.2 18.2 %copy-start.43 = (f32[1024]{0:T(1024)}, f32[1024]{0:T(1024)S(1)}, u32[]{:S(2)}) copy-start(f32[1024]{0:T(1024)S(1)} %broadcast_multiply_fusion.1) | copy-start | bytes 12292
  524.2 362.6 %reduce-scatter.8.cloned.1.call-start = ((), (), s32[]{:S(2)}) async-start(), calls=%async_computation.7 | async-start | bytes 3342336 | tf_op jit(solution)/shard_map/reduce_scatter | solution.py:284
  528.5 155.0 %copy-start.30 = (f32[1024,32]{0,1:T(8,128)S(1)}, f32[1024,32]{0,1:T(8,128)}, u32[]{:S(2)}) copy-start(f32[1024,32]{0,1:T(8,128)} %copy-done.29) | copy-start | bytes 393220
  528.5 155.0 %copy-start.35 = (f32[1024,32]{0,1:T(8,128)S(1)}, f32[1024,32]{0,1:T(8,128)}, u32[]{:S(2)}) copy-start(f32[1024,32]{0,1:T(8,128)} %get-tuple-element.392) | copy-start | bytes 393220
  683.6 33.9 %copy-start.4 = (bf16[12,1024,64]{1,2,0:T(8,128)(2,1)}, bf16[12,1024,64]{1,2,0:T(8,128)(2,1)S(1)}, u32[]{:S(2)}) copy-start(bf16[12,1024,64]{1,2,0:T(8,128)(2,1)S(1)} %get-tuple-element.119) | copy-start | bytes 4718596
  702.5 263.8 %reduce-scatter.10.cloned.1.call-start = ((), (), s32[]{:S(2)}) async-start(), calls=%async_computation.8 | async-start | bytes 3342336 | tf_op jit(solution)/shard_map/reduce_scatter | solution.py:284
  717.0 384.1 %reduce-scatter.12.cloned.1.call-start = ((), (), s32[]{:S(2)}) async-start(), calls=%async_computation.9 | async-start | bytes 3342336 | tf_op jit(solution)/shard_map/reduce_scatter | solution.py:284
  727.8 523.0 %reduce-scatter.20.cloned.1.call-start = ((), (), s32[]{:S(2)}) async-start(), calls=%async_computation.13 | async-start | bytes 6684672 | tf_op jit(solution)/shard_map/reduce_scatter | solution.py:223
  754.5 646.5 %reduce-scatter.18.cloned.1.call-start = ((), (), s32[]{:S(2)}) async-start(), calls=%async_computation.12 | async-start | bytes 6684672 | tf_op jit(solution)/shard_map/reduce_scatter | solution.py:217
  779.1 771.7 %reduce-scatter.16.cloned.1.call-start = ((), (), s32[]{:S(2)}) async-start(), calls=%async_computation.11 | async-start | bytes 6684672 | tf_op jit(solution)/shard_map/reduce_scatter | solution.py:211
  802.7 75.9 %copy-start.23 = (bf16[1024,12,64]{0,2,1:T(8,128)(2,1)S(1)}, bf16[1024,12,64]{0,2,1:T(8,128)(2,1)}, u32[]{:S(2)}) copy-start(bf16[1024,12,64]{0,2,1:T(8,128)(2,1)} %copy-done.22) | copy-start | bytes 4718596
  802.7 75.9 %copy-start.32 = (bf16[768,768]{0,1:T(8,128)(2,1)S(1)}, bf16[768,768]{0,1:T(8,128)(2,1)}, u32[]{:S(2)}) copy-start(bf16[768,768]{0,1:T(8,128)(2,1)} %reshape.302) | copy-start | bytes 3538948
  802.7 771.0 %all-reduce.10.cloned.1.call-start = ((), (), s32[]{:S(2)}) async-start(), calls=%async_computation.21 | async-start | bytes 1966080 | tf_op jit(solution)/shard_map/psum | solution.py:290
  885.1 671.8 %copy-start.1 = (f32[1024,768]{0,1:T(8,128)S(1)}, f32[1024,768]{0,1:T(8,128)}, u32[]{:S(2)}) copy-start(f32[1024,768]{0,1:T(8,128)} %copy-done) | copy-start | bytes 9437188
  885.1 671.8 %copy-start.37 = (f32[768]{0:T(1024)S(1)}, f32[768]{0:T(1024)}, u32[]{:S(2)}) copy-start(f32[768]{0:T(1024)} %copy-done.36) | copy-start | bytes 9220
  885.1 671.8 %copy-start.39 = (f32[1024]{0:T(1024)S(1)}, f32[1024]{0:T(1024)}, u32[]{:S(2)}) copy-start(f32[1024]{0:T(1024)} %copy-done.38) | copy-start | bytes 12292
  885.1 671.8 %copy-start.41 = (f32[1024]{0:T(1024)S(1)}, f32[1024]{0:T(1024)}, u32[]{:S(2)}) copy-start(f32[1024]{0:T(1024)} %copy-done.40) | copy-start | bytes 12292
  (33 other events, 99.1 us)
Sparse Core Ops, SparseCore 0:
  10.9 60.7 all-gather.18
  74.4 56.6 all-gather.16
  134.0 56.6 all-gather.20
  193.4 56.6 all-gather.22
  252.7 66.7 all-gather.24
  322.2 66.5 all-gather.26
  391.5 69.6 all-gather.28
  524.4 128.8 reduce-scatter.13
  702.6 128.9 reduce-scatter.7
  836.5 129.8 reduce-scatter.9
  971.3 129.7 reduce-scatter.11
  1106.2 144.5 reduce-scatter.19
  1256.0 144.9 reduce-scatter.17
  1406.1 144.6 reduce-scatter.15
  1554.6 19.0 all-reduce.9
where the time goes:
time: 1600 us; the launch traced here: 1590 us
  waiting for transfers between devices  941 us (59%)
  matrix products  290 us (18%)
  local copies, waits for them, and re-layouts  157 us (10%)
  blocking collectives  122 us (8%)
  other arithmetic  64.3 us (4%)
    reduce_scatter x4, waiting for transfers between devices, on_device(): lax.psum_scatter(attention_parts + (first_lanes,), ('row', 'col'), scatte...  211 us
    reduce_scatter x1, waiting for transfers between devices, on_device(): lax.psum_scatter(disassemble(up_term, grid_rows, grid_cols), ('row', 'col...  148 us
    reduce_scatter x1, waiting for transfers between devices, on_device(): lax.psum_scatter(disassemble(down_term, grid_rows, grid_cols), ('row', 'c...  148 us
    reduce_scatter x1, waiting for transfers between devices, on_device(): lax.psum_scatter(disassemble(gate_term, grid_rows, grid_cols), ('row', 'c...  148 us
    unnamed x2, blocking collectives  119 us
    all_gather x1, waiting for transfers between devices, fetch_feedforward(): lax.all_gather(down_weight[None], ('row', 'col'), axis=0, tiled=True)  65.5 us
    all_gather x1, waiting for transfers between devices, fetch_feedforward(): lax.all_gather(up_weight[None], ('row', 'col'), axis=0, tiled=True)  62.2 us
    all_gather x1, waiting for transfers between devices, fetch_attention(): lax.all_gather(query_weight[None], ('row', 'col'), axis=0, tiled=True)  50 us
  transfers between devices with their start and end apart: 15, of which 12 were waited for; matrix products, arithmetic and copies ran while one was open for 27% of the time, Pallas kernels for 0%

commit v1 on v0

--- a/solution.py
+++ b/solution.py
@@ -7,6 +7,27 @@
 EPSILON = 1e-06
 ROPE_BASE = 10000.0
 NEGATIVE = -1e30
+
+
+def ring_gather(x, axis, dim):
+    size, index, rows = (lax.axis_size(axis), lax.axis_index(axis), x.shape[dim])
+    right = [(i, (i + 1) % size) for i in range(size)]
+    backward = [(i, (i - 1) % size) for i in range(size)]
+    whole = jnp.zeros((*x.shape[:dim], size * rows, *x.shape[dim + 1 :]), x.dtype)
+    whole = lax.dynamic_update_slice_in_dim(whole, x, index * rows, axis=dim)
+    from_left = from_right = x
+    middle = size // 2
+    for turn in range(1, middle + 1):
+        from_left = lax.ppermute(from_left, axis, right)
+        whole = lax.dynamic_update_slice_in_dim(
+            whole, from_left, (index - turn) % size * rows, axis=dim
+        )
+        if turn < size - middle:
+            from_right = lax.ppermute(from_right, axis, backward)
+            whole = lax.dynamic_update_slice_in_dim(
+                whole, from_right, (index + turn) % size * rows, axis=dim
+            )
+    return whole
 
 
 def for_sending(value):
@@ -54,7 +75,7 @@
 def fetch_feedforward(gate_weight, up_weight, down_weight, second_gain, grid_rows, grid_cols):
     pieces = (
         lax.all_gather(gate_weight[None], ("row", "col"), axis=0, tiled=True),
-        lax.all_gather(up_weight[None], ("row", "col"), axis=0, tiled=True),
+        ring_gather(up_weight[None], ("row", "col"), 0),
         lax.all_gather(down_weight[None], ("row", "col"), axis=0, tiled=True),
         lax.all_gather(second_gain[None], ("row", "col"), axis=0, tiled=True),
     )

time: 1600 us -> 1550 us (0.969)
  waiting for transfers between devices: 941 us -> 855 us
  starting transfers between devices: 1.17 us -> 36.7 us
    all_gather x1 -> x0, waiting for transfers between devices: 62.2 us -> none  [fetch_feedforward(): lax.all_gather(up_weight[None], ('row', 'col'), axis=0, tiled=True)]
    all_gather x1, waiting for transfers between devices: 50 us -> 0.01 us  [fetch_attention(): lax.all_gather(query_weight[None], ('row', 'col'), axis=0, tiled=True)]
    ppermute x0 -> x15, waiting for transfers between devices: none -> 45.1 us  [the longest x8 24 us: ring_gather(): from_left = lax.ppermute(from_left, axis, right)]
    ppermute x0 -> x15, starting transfers between devices: none -> 35.5 us  [the longest x7 24.3 us: ring_gather(): from_right = lax.ppermute(from_right, axis, backward)]
    unnamed x114 -> x116, local copies, waits for them, and re-layouts: 33.5 us -> 33.6 us
  transfers between devices with their start and end apart: 15 -> 29, of which waited for: 12 -> 21; matrix products, arithmetic and copies ran while one was open for 27% -> 28% of each run, Pallas kernels for 0% -> 0%
where the time goes in v1:
time: 1550 us; the launch traced here: 1540 us
  waiting for transfers between devices  855 us (55%)
  matrix products  291 us (19%)
  local copies, waits for them, and re-layouts  158 us (10%)
  blocking collectives  116 us (7%)
  other arithmetic  64.3 us (4%)
  starting transfers between devices  36.7 us (2%)
  between operations  15.9 us (1%)
    reduce_scatter x4, waiting for transfers between devices, on_device(): lax.psum_scatter(attention_parts + (first_lanes,), ('row', 'col'), scatte...  211 us
    reduce_scatter x1, waiting for transfers between devices, on_device(): lax.psum_scatter(disassemble(down_term, grid_rows, grid_cols), ('row', 'c...  149 us
    reduce_scatter x1, waiting for transfers between devices, on_device(): lax.psum_scatter(disassemble(gate_term, grid_rows, grid_cols), ('row', 'c...  149 us
    reduce_scatter x1, waiting for transfers between devices, on_device(): lax.psum_scatter(disassemble(up_term, grid_rows, grid_cols), ('row', 'col...  148 us
    unnamed x2, blocking collectives  113 us
    all_gather x1, waiting for transfers between devices, fetch_feedforward(): lax.all_gather(down_weight[None], ('row', 'col'), axis=0, tiled=True)  65.3 us
    all_gather x1, waiting for transfers between devices, fetch_feedforward(): lax.all_gather(gate_weight[None], ('row', 'col'), axis=0, tiled=True)  48 us
    dot_general x7, matrix products, back_product(): jnp.einsum('tb,ab->ta', grad, weight, preferred_element_type=jnp.float32)  39.5 us
  transfers between devices with their start and end apart: 29, of which 21 were waited for; matrix products, arithmetic and copies ran while one was open for 28% of the time, Pallas kernels for 0%

profile of v1, /device:TPU:0, one launch (start us, length us, event | category | flops | bytes accessed | tf_op | source)
XLA Modules:
  0.0 1537.1 jit_solution(10068132202937804274)
XLA Ops:
  24.3 38.8 %all-reduce.5 = (bf16[768]{0:T(1024)(128)(2,1)S(1)}, bf16[768]{0:T(1024)(128)(2,1)S(1)}) all-reduce(bf16[768]{0:T(1024)(128)(2,1)S(1)} %dynamic-update-slice, bf16[768]{0:T(1024)(128)(2,1)S(1)} %dynamic-update-slice.1), channel_id=6, replica_groups=mesh['dp'=2,'row'=4,'col'=4] {'row','col'}, use_global_device_ids=true, to_apply=%add | all-reduce | flops 1536 | bytes 6144
  66.6 5.4 collective-permute-start.3
  77.1 6.0 collective-permute-start.5
  106.0 8.7 collective-permute-done.9
  128.2 5.3 collective-permute-start.14
  135.5 6.6 collective-permute-done.14
  172.3 31.8 %all-gather.19.cloned.1.call-done = bf16[3072,192]{1,0:T(8,128)(2,1)} async-done(((bf16[192,192]{1,0:T(8,128)(2,1)}), bf16[3072,192]{1,0:T(8,128)(2,1)}) %all-gather.19.cloned.1.call-update) | async-done | bytes 1179664 | tf_op jit(solution)/shard_map/all_gather | solution.py:67
  216.9 56.9 %while.32 = (s32[]{:T(128)}, bf16[12,1024,64]{1,2,0:T(8,128)(2,1)S(1)}, f32[12,1024]{1,0:T(8,128)S(1)}, f32[12,1024]{1,0:T(8,128)S(1)}, bf16[12,1024,64]{2,1,0:T...) while((s32[]{:T(128)}, ...), condition=%wide.region_4.5_spmd.clone.clone, body=%wide.region_1.4_spmd.clone.sunk.clone | while | flops 279967744 | bytes 13678685 | solution.py:191
  285.0 48.0 %all-gather.23.cloned.1.call-done = bf16[3072,512]{1,0:T(8,128)(2,1)} async-done(((bf16[192,512]{1,0:T(8,128)(2,1)}), bf16[3072,512]{1,0:T(8,128)(2,1)}) %all-gather.23.cloned.1.call-update) | async-done | bytes 3145744 | tf_op jit(solution)/shard_map/all_gather | solution.py:77
  340.0 65.3 %all-gather.25.cloned.1.call-done = bf16[8192,192]{0,1:T(8,128)(2,1)} async-done(((bf16[512,192]{0,1:T(8,128)(2,1)}), bf16[8192,192]{0,1:T(8,128)(2,1)}) %all-gather.25.cloned.1.call-update) | async-done | bytes 3145744 | tf_op jit(solution)/shard_map/all_gather | solution.py:79
  405.3 6.5 reshape.314
  420.9 7.9 multiply_convert_fusion.3
  428.8 5.7 multiply_reduce_fusion.3
  437.3 12.6 multiply_convert_fusion.1
  450.0 5.5 fusion.74
  472.8 155.3 %while.33 = (s32[]{:T(128)}, f32[12,1024,64]{1,2,0:T(8,128)}, f32[12,1024,64]{1,2,0:T(8,128)}, bf16[12,1024,64]{1,2,0:T(8,128)(2,1)S(1)}, bf16[12,1024,64]{2,1,0...) while((s32[]{:T(128)}, f32[12,1024,64]{1,2,0:T(8,128)}, ...), condition=%wide.region_11.12_spmd.clone.clone, body=%wide.region_9.11_spmd.clone.sunk.clone | while | flops 689961984 | bytes 34129008 | solution.py:267
  673.9 9.3 fusion.58
  683.2 8.5 reshape.328
  691.7 7.5 copy.147
  700.6 7.4 fusion.79
  708.0 8.4 reshape.326
  716.5 7.3 copy.145
  723.9 7.5 fusion.78
  731.3 8.4 reshape.324
  739.8 7.7 copy.144
  748.2 74.1 %all-reduce.4 = (bf16[16,48]{1,0:T(8,128)(2,1)S(1)}, bf16[16,48]{1,0:T(8,128)(2,1)S(1)}) all-reduce(f32[16,48]{1,0:T(8,128)S(1)} %reshape.330, f32[16,48]{1,0:T(8,128)S(1)} %reshape.331), channel_id=17, replica_groups=mesh['dp'=2,'row'=4,'col'=4] {'row','col'}, use_global_device_ids=true, to_apply=%region_27.28.clone | all-reduce | flops 1536 | bytes 9216
  832.6 78.4 %reduce-scatter.10.cloned.1.call-done = f32[1,192,192]{2,1,0:T(8,128)} async-done(((f32[16,192,192]{2,1,0:T(8,128)}), f32[1,192,192]{2,1,0:T(8,128)}) %reduce-scatter.10.cloned.1.call-update) | async-done | bytes 147472 | tf_op jit(solution)/shard_map/reduce_scatter | solution.py:305
  912.6 133.0 %reduce-scatter.12.cloned.1.call-done = f32[1,192,192]{2,1,0:T(8,128)} async-done(((f32[16,192,192]{2,1,0:T(8,128)}), f32[1,192,192]{2,1,0:T(8,128)}) %reduce-scatter.12.cloned.1.call-update) | async-done | bytes 147472 | tf_op jit(solution)/shard_map/reduce_scatter | solution.py:305
  1047.2 148.7 %reduce-scatter.20.cloned.1.call-done = f32[1,512,192]{1,2,0:T(8,128)} async-done(((f32[16,512,192]{1,2,0:T(8,128)}), f32[1,512,192]{1,2,0:T(8,128)}) %reduce-scatter.20.cloned.1.call-update) | async-done | bytes 393232 | tf_op jit(solution)/shard_map/reduce_scatter | solution.py:244
  1197.6 148.2 %reduce-scatter.18.cloned.1.call-done = f32[1,192,512]{2,1,0:T(8,128)} async-done(((f32[16,192,512]{2,1,0:T(8,128)}), f32[1,192,512]{2,1,0:T(8,128)}) %reduce-scatter.18.cloned.1.call-update) | async-done | bytes 393232 | tf_op jit(solution)/shard_map/reduce_scatter | solution.py:238
  1347.4 148.5 %reduce-scatter.16.cloned.1.call-done = f32[1,192,512]{2,1,0:T(8,128)} async-done(((f32[16,192,512]{2,1,0:T(8,128)}), f32[1,192,512]{2,1,0:T(8,128)}) %reduce-scatter.16.cloned.1.call-update) | async-done | bytes 393232 | tf_op jit(solution)/shard_map/reduce_scatter | solution.py:232
  1502.0 7.9 add_convert_fusion
  (412 shorter events, 455.1 us)
Async XLA Ops:
  7.2 140.2 %all-gather.17.cloned.1.call-start = ((), (), s32[]{:S(2)}) async-start(), calls=%async_computation.15 | async-start | bytes 1671168 | tf_op jit(solution)/shard_map/all_gather | solution.py:66
  7.9 149.3 %all-gather.15.cloned.1.call-start = ((), (), s32[]{:S(2)}) async-start(), calls=%async_computation.14 | async-start | bytes 1671168 | tf_op jit(solution)/shard_map/all_gather | solution.py:65
  8.7 195.4 %all-gather.19.cloned.1.call-start = ((), (), s32[]{:S(2)}) async-start(), calls=%async_computation.16 | async-start | bytes 1671168 | tf_op jit(solution)/shard_map/all_gather | solution.py:67
  9.4 264.5 %all-gather.21.cloned.1.call-start = ((), (), s32[]{:S(2)}) async-start(), calls=%async_computation.17 | async-start | bytes 1671168 | tf_op jit(solution)/shard_map/all_gather | solution.py:68
  10.0 323.0 %all-gather.23.cloned.1.call-start = ((), (), s32[]{:S(2)}) async-start(), calls=%async_computation.18 | async-start | bytes 3342336 | tf_op jit(solution)/shard_map/all_gather | solution.py:77
  10.6 394.7 %all-gather.25.cloned.1.call-start = ((), (), s32[]{:S(2)}) async-start(), calls=%async_computation.19 | async-start | bytes 3342336 | tf_op jit(solution)/shard_map/all_gather | solution.py:79
  10.6 55.8 %collective-permute-start = (bf16[1,192,512]{2,1,0:T(8,128)(2,1)}, bf16[1,192,512]{2,1,0:T(8,128)(2,1)}, u32[]{:S(2)}, u32[]{:S(2)}) collective-permute-start(bf16[1,192,512]{2,1,0:T(8,128)(2,1)} %bitcast.334), channel_id=1, source_target_pairs={{0,1},{1,2},{2,3},{3,4},{4,5},{5,6},{6,7},{7,8},{8,9},{9,10},{10,1... | collective-permute-start | bytes 589832 | tf_op jit(solution)/shard_map/ppermute | solution.py:21
  13.7 52.9 %collective-permute-start.1 = (bf16[1,192,512]{2,1,0:T(8,128)(2,1)}, bf16[1,192,512]{2,1,0:T(8,128)(2,1)}, u32[]{:S(2)}, u32[]{:S(2)}) collective-permute-start(bf16[1,192,512]{2,1,0:T(8,128)(2,1)} %bitcast.335), channel_id=1, source_target_pairs={{0,15},{1,0},{2,1},{3,2},{4,3},{5,4},{6,5},{7,6},{8,7},{9,8},{10,9... | collective-permute-start | bytes 589832 | tf_op jit(solution)/shard_map/ppermute | solution.py:26
  17.7 811.6 %reduce-scatter.14.cloned.1.call-start = ((), (), s32[]{:S(2)}) async-start(), calls=%async_computation.10 | async-start | bytes 3342336 | tf_op jit(solution)/shard_map/reduce_scatter | solution.py:305
  66.4 10.7 collective-permute-start.2
  66.6 10.5 collective-permute-start.3
  77.1 9.4 collective-permute-start.4
  77.1 11.6 collective-permute-start.5
  86.5 10.1 collective-permute-start.6
  88.7 12.8 collective-permute-start.7
  96.6 9.4 collective-permute-start.8
  101.4 13.3 collective-permute-start.9
  106.0 10.7 collective-permute-start.10
  114.7 8.0 collective-permute-start.11
  116.7 11.4 collective-permute-start.12
  122.7 12.8 collective-permute-start.13
  128.2 14.0 collective-permute-start.14
  468.5 362.6 %reduce-scatter.8.cloned.1.call-start = ((), (), s32[]{:S(2)}) async-start(), calls=%async_computation.7 | async-start | bytes 3342336 | tf_op jit(solution)/shard_map/reduce_scatter | solution.py:305
  647.1 263.9 %reduce-scatter.10.cloned.1.call-start = ((), (), s32[]{:S(2)}) async-start(), calls=%async_computation.8 | async-start | bytes 3342336 | tf_op jit(solution)/shard_map/reduce_scatter | solution.py:305
  661.7 383.9 %reduce-scatter.12.cloned.1.call-start = ((), (), s32[]{:S(2)}) async-start(), calls=%async_computation.9 | async-start | bytes 3342336 | tf_op jit(solution)/shard_map/reduce_scatter | solution.py:305
  672.5 523.3 %reduce-scatter.20.cloned.1.call-start = ((), (), s32[]{:S(2)}) async-start(), calls=%async_computation.13 | async-start | bytes 6684672 | tf_op jit(solution)/shard_map/reduce_scatter | solution.py:244
  699.2 646.5 %reduce-scatter.18.cloned.1.call-start = ((), (), s32[]{:S(2)}) async-start(), calls=%async_computation.12 | async-start | bytes 6684672 | tf_op jit(solution)/shard_map/reduce_scatter | solution.py:238
  723.8 772.1 %reduce-scatter.16.cloned.1.call-start = ((), (), s32[]{:S(2)}) async-start(), calls=%async_computation.11 | async-start | bytes 6684672 | tf_op jit(solution)/shard_map/reduce_scatter | solution.py:232
  747.5 771.4 %all-reduce.10.cloned.1.call-start = ((), (), s32[]{:S(2)}) async-start(), calls=%async_computation.20 | async-start | bytes 1966080 | tf_op jit(solution)/shard_map/psum | solution.py:311
  829.3 672.7 %copy-start.38 = (f32[768]{0:T(1024)S(1)}, f32[768]{0:T(1024)}, u32[]{:S(2)}) copy-start(f32[768]{0:T(1024)} %copy-done.37) | copy-start | bytes 9220
  829.3 672.7 %copy-start.40 = (f32[1024]{0:T(1024)S(1)}, f32[1024]{0:T(1024)}, u32[]{:S(2)}) copy-start(f32[1024]{0:T(1024)} %copy-done.39) | copy-start | bytes 12292
  829.3 672.7 %copy-start.42 = (f32[1024]{0:T(1024)S(1)}, f32[1024]{0:T(1024)}, u32[]{:S(2)}) copy-start(f32[1024]{0:T(1024)} %copy-done.41) | copy-start | bytes 12292
  (48 other events, 2209.0 us)
Sparse Core Ops, SparseCore 0:
  10.9 66.0 all-gather.16
  79.7 64.1 all-gather.14
  146.8 57.2 all-gather.18
  206.8 56.6 all-gather.20
  266.2 66.8 all-gather.22
  335.6 69.6 all-gather.24
  468.6 128.6 reduce-scatter.13
  647.2 128.7 reduce-scatter.7
  781.0 129.9 reduce-scatter.9
  915.8 129.7 reduce-scatter.11
  1050.8 144.9 reduce-scatter.19
  1200.9 144.7 reduce-scatter.17
  1350.9 144.9 reduce-scatter.15
  1499.8 19.0 all-reduce.9
